TPU v7x, 32 devices: a whole 2x2x4 slice. The times are simulated.
32 devices in a mesh: cfd: 8 (over z, core), panel: 2 (over y), obs: 2 (over x).
Axes of the slice: x: 2, y: 2, z: 4, core: 2. Of those that a mesh axis runs over, the one named last changes fastest.
Arguments:
- state: float32 [5, 64, 32, 256], P(None, 'cfd', 'panel', 'obs'), may hold values from -6 to 6
- mean_speed: float32 [64, 32, 256], P('cfd', 'panel', 'obs'), may hold values from 0 to 0.9
- eddy_visc: float32 [64, 32, 256], P('cfd', 'panel', 'obs'), may hold values from 0.02 to 0.5
- panel_cell: int32 [8, 2, 2, 8, 4], P('cfd', 'panel', 'obs'), may hold values from 0 to 16383
- panel_count: int32 [8, 2, 2, 8], P('cfd', 'panel', 'obs'), may hold values from 0 to 4, as said below
- weights: bfloat16 [16, 2, 8, 4, 2, 2, 64], P(('cfd', 'panel'), None, None, None, None, 'obs'), may hold values from -1.5 to 1.5
- delays: int32 [16, 2, 8, 2, 1], P(('cfd', 'panel'), None, None, 'obs'), may hold values from 0 to 124
Outputs:
- flow_out: float32 [5, 64, 32, 256], P(None, 'cfd', 'panel', 'obs')
- observer_pressure: float32 [2, 64, 128], P('obs', ('cfd', 'panel'))
Inputs may be any that keep to these rules, and one draw needn't show every extreme that they name: `panel_cell`: A flat cell index within one flow block of 8 x 16 x 128 cells. `panel_count`: in every flow block some destination shard gets all 4 slots, and for each pair of second and third block indices that is the same shard for all blocks along the first dimension.
All inputs are finite; a program needn't handle non-finite values.
Results may differ from a plain program's by a relative error of at most 0.0029.
Values may be sent and summed in bfloat16 or wider, within the bound.
A program may use at most 64 MiB of HBM per device.

v0:
```python
import functools

import jax
import jax.numpy as jnp
from jax import lax
from jax.experimental import pallas as pl
from jax.experimental.pallas import tpu as pltpu
from jax.sharding import PartitionSpec as P

STEPS = 4
TIME_STEP = 0.2
PAD = 8
AXES = ("cfd", "panel", "obs")


def window_kernel(
    sizes,
    cells,
    counts,
    late_bins,
    state,
    speed,
    visc,
    weights,
    flow_out,
    heard_out,
    s_ref,
    hx_ref,
    hy_ref,
    ys_ref,
    m_ref,
    v_ref,
    vy_ref,
    vz_ref,
    zs_ref,
    zr_ref,
    raw_ref,
    g_ref,
    hot_ref,
    sig_ref,
    parcel_ref,
    w_ref,
    wt_ref,
    late_ref,
    early_ref,
    part_ref,
    gather_ref,
    load_sem,
    send_sem,
    recv_sem,
    w_sem,
    r_sem,
):
    span = dict(zip(AXES, sizes))
    cx, cy, cz = speed.shape
    rows = cx * cy
    me = {axis: lax.axis_index(axis) for axis in AXES}
    has = {}
    for axis in AXES:
        has[axis, 1] = me[axis] < span[axis] - 1
        has[axis, -1] = me[axis] > 0
    total = sizes[0] * sizes[1] * sizes[2]
    assert sizes[2] == 2
    low = me["obs"] > 0
    near = sum(sizes) - 3 <= 3 * (STEPS - 1)

    loads = [
        pltpu.make_async_copy(
            state, s_ref.at[0, :, :, pl.ds(PAD, cy), :], load_sem.at[0]
        ),
        pltpu.make_async_copy(speed, m_ref, load_sem.at[1]),
        pltpu.make_async_copy(visc, v_ref, load_sem.at[2]),
        pltpu.make_async_copy(weights, raw_ref, load_sem.at[3]),
    ]
    for load in loads:
        load.start()

    def place(index):
        return {
            "cfd": index // (sizes[1] * sizes[2]),
            "panel": (index // sizes[2]) % sizes[1],
            "obs": index % sizes[2],
        }

    my_index = (me["cfd"] * sizes[1] + me["panel"]) * sizes[2] + me["obs"]
    barrier = pltpu.get_barrier_semaphore()
    if near:
        met = jnp.int32(0)
        for axis in AXES:
            for way in (1, -1):

                @pl.when(has[axis, way])
                def _():
                    pl.semaphore_signal(
                        barrier,
                        inc=1,
                        device_id={**me, axis: me[axis] + way},
                        device_id_type=pl.DeviceIdType.MESH,
                    )

                met = met + has[axis, way].astype(jnp.int32)
        pl.semaphore_wait(barrier, met)
    else:

        @pl.loop(1, total)
        def _(hop):
            pl.semaphore_signal(
                barrier,
                inc=1,
                device_id=place((my_index + hop) % total),
                device_id_type=pl.DeviceIdType.MESH,
            )

        pl.semaphore_wait(barrier, total - 1)

    line = jnp.zeros((3, s_ref.shape[1], cx, 1, cz), jnp.float32)
    s_ref[:, :, :, PAD - 1 : PAD, :] = line
    s_ref[:, :, :, PAD + cy : PAD + cy + 1, :] = line
    for axis, halo in (("cfd", hx_ref), ("panel", hy_ref)):
        for side, way in enumerate((-1, 1)):

            @pl.when(jnp.logical_not(has[axis, way]))
            def _():
                halo[:, side] = jnp.zeros((3,) + halo.shape[2:], jnp.float32)

    zs_ref[...] = jnp.zeros(zs_ref.shape, jnp.float32)

    def route(buf, axis, way):
        side = 0 if way == 1 else 1
        if axis == "cfd":
            src = s_ref.at[buf, :, cx - 1 if way == 1 else 0, pl.ds(PAD, cy), :]
            dst = hx_ref.at[buf, side]
        elif axis == "panel":
            src = ys_ref.at[buf, 1 - side]
            dst = hy_ref.at[buf, side]
        else:
            src = zs_ref.at[buf]
            dst = zr_ref.at[buf]
        lane = 2 * AXES.index(axis) + (way == 1)
        return pltpu.make_async_remote_copy(
            src_ref=src,
            dst_ref=dst,
            send_sem=send_sem.at[buf, lane],
            recv_sem=recv_sem.at[buf, lane],
            device_id={**me, axis: me[axis] + way},
            device_id_type=pl.DeviceIdType.MESH,
        )

    def send(buf, axes):
        for axis in axes:
            for way in (1, -1):

                @pl.when(has[axis, way])
                def _():
                    route(buf, axis, way).start()

    def settle(buf):
        for axis in AXES:
            for way in (1, -1):

                @pl.when(has[axis, -way])
                def _():
                    route(buf, axis, way).wait_recv()

        for axis in AXES:
            for way in (1, -1):

                @pl.when(has[axis, way])
                def _():
                    route(buf, axis, way).wait_send()

    lane_id = lax.broadcasted_iota(jnp.int32, (cy, cz), 1)
    row_id = lax.broadcasted_iota(jnp.int32, (cy, cz), 0)
    fields = s_ref.shape[1]

    assert fields * cx <= cz

    def rim_lane(value):
        return jnp.where(low, value[:, 0:1], value[:, cz - 1 : cz])

    def collect(packed, x, f, value):
        spot = f * cx + x
        return jnp.where(lane_id == spot, pltpu.roll(value, spot + 1 - me["obs"], 1), packed)

    def pack_sides(buf):
        for f in range(fields):
            for side, row in enumerate((PAD, PAD + cy - 1)):
                ys_ref[buf, side, f] = s_ref[buf, f, :, row, :]

    def blank():
        return jnp.zeros((cy, cz), jnp.float32)

    half = 0.5 * TIME_STEP

    def bulk(src, dst, number):
        packed = blank()
        for x in range(cx):
            visc_h = v_ref[x]
            speed_h = m_ref[x]
            mid, moved, ups, across, along = [], [], {}, {}, []
            for f in range(fields):
                c = s_ref[src, f, x, PAD : PAD + cy, :]
                n = s_ref[src, f, x, PAD + 1 : PAD + cy + 1, :]
                s = s_ref[src, f, x, PAD - 1 : PAD + cy - 1, :]
                u = jnp.where(lane_id == cz - 1, 0.0, pltpu.roll(c, cz - 1, 1))
                d = jnp.where(lane_id == 0, 0.0, pltpu.roll(c, 1, 1))
                if x == 0:
                    dx = sx = s_ref[src, f, x + 1, PAD : PAD + cy, :]
                elif x == cx - 1:
                    sx = s_ref[src, f, x - 1, PAD : PAD + cy, :]
                    dx = -sx
                else:
                    e = s_ref[src, f, x + 1, PAD : PAD + cy, :]
                    w = s_ref[src, f, x - 1, PAD : PAD + cy, :]
                    dx, sx = e - w, e + w
                spread = sx + (n + s) + (u + d) - 6.0 * c
                mid.append(c)
                along.append(dx)
                moved.append(visc_h * spread - speed_h * dx)
                if f in (2, 4):
                    across[f] = n - s
                if f in (3, 4):
                    ups[f] = u - d
            diverge = half * (along[1] + across[2] + ups[3])
            forcing = [diverge, half * along[4], half * across[4], half * ups[4], diverge]
            for f in range(fields):
                value = mid[f] + (moved[f] - forcing[f])
                if number == 1:
                    value = 0.75 * s_ref[0, f, x, PAD : PAD + cy, :] + 0.25 * value
                elif number == 2:
                    value = s_ref[0, f, x, PAD : PAD + cy, :] * (1.0 / 3.0) + (2.0 / 3.0) * value
                s_ref[dst, f, x, PAD : PAD + cy, :] = value
                packed = collect(packed, x, f, value)
        zs_ref[dst] = packed
        pack_sides(dst)

    sub_id = lax.broadcasted_iota(jnp.int32, (8, cz), 0)

    def push(halo, coef, way, normal, scale):
        sent = -way * half * scale
        base = [(scale * coef) * value for value in halo]
        cross = sent * halo[normal]
        base[0] = base[0] + cross
        base[4] = base[4] + cross
        base[normal] = base[normal] + sent * halo[4]
        return base

    def correct(src, dst, number):
        scale = (1.0, 0.25, 2.0 / 3.0)[number]
        south, north = [
            push([hy_ref[src, side, f] for f in range(fields)], vy_ref[side], way, 2, scale)
            for side, way in enumerate((-1, 1))
        ]
        faces = {}
        for x, side, way in ((0, 0, -1), (cx - 1, 1, 1)):
            coef = v_ref[x] - way * m_ref[x]
            faces[x] = push([hx_ref[src, side, f] for f in range(fields)], coef, way, 1, scale)
        spot = lax.broadcasted_iota(jnp.int32, (cx, cz), 1)
        step_id = lax.broadcasted_iota(jnp.int32, (cx, cz), 0)
        end = jnp.where(low, 0, cz - 1)
        sent = jnp.where(low, half * scale, -half * scale)
        held = zr_ref[src]
        cross = jnp.where(
            lane_id < cx,
            pltpu.roll(held, cz - 3 * cx, 1),
            jnp.where(lane_id < 4 * cx, pltpu.roll(held, cz - cx, 1), pltpu.roll(held, cx, 1)),
        )
        crossed = (lane_id < cx) | ((lane_id >= 3 * cx) & (lane_id < 5 * cx))
        fix = (scale * vz_ref[...]) * held + sent * jnp.where(crossed, cross, 0.0)
        tall = jnp.zeros((cy, cz), jnp.float32)
        for x in (0, cx - 1):
            for f in range(fields):
                tall = collect(tall, x, f, faces[x][f])
        rows_out = []
        for own in (south, north):
            wide = jnp.zeros((cx, cz), jnp.float32)
            for f in range(fields):
                wide = jnp.where(spot == step_id + f * cx, rim_lane(own[f]), wide)
            rows_out.append(jnp.sum(wide, axis=0, keepdims=True))
        tall = tall + jnp.where(row_id == 0, rows_out[0], 0.0)
        tall = tall + jnp.where(row_id == cy - 1, rows_out[1], 0.0)
        zs_ref[dst] = zs_ref[dst] + (fix + tall)
        yield "obs"
        turned = jnp.transpose(fix)
        for side, (own, row) in enumerate(((south, 0), (north, cy - 1))):
            for f in range(fields):
                ends = turned[f * cx : (f + 1) * cx, row : row + 1]
                side_fix = own[f] + jnp.where(spot == end, ends, 0.0)
                for x in (0, cx - 1):
                    side_fix = side_fix + jnp.where(step_id == x, faces[x][f][row : row + 1, :], 0.0)
                ys_ref[dst, side, f] = ys_ref[dst, side, f] + side_fix
        yield "panel"
        for place_x, x in enumerate([0, cx - 1] + list(range(1, cx - 1))):
            for f in range(fields):
                rim = [jnp.where(sub_id == 0, south[f][x : x + 1, :], 0.0)]
                if cy > 16:
                    rim.append(jnp.zeros((cy - 16, cz), jnp.float32))
                rim.append(jnp.where(sub_id == 7, north[f][x : x + 1, :], 0.0))
                edge = jnp.where(lane_id == end, fix[:, f * cx + x : f * cx + x + 1], 0.0)
                value = s_ref[dst, f, x, PAD : PAD + cy, :] + (
                    jnp.concatenate(rim, axis=0) + edge
                )
                if x in faces:
                    value = value + faces[x][f]
                s_ref[dst, f, x, PAD : PAD + cy, :] = value
            if place_x == 1:
                yield "cfd"

    cap, groups = cells.shape
    slots = cap * groups

    def mark():
        lane = lax.broadcasted_iota(jnp.int32, (2, cz), 1)

        def body(slot, carry):
            rank, group = lax.rem(slot, cap), lax.div(slot, cap)
            spot = jnp.where(rank < counts[group], lax.rem(cells[rank, group], cz), -1)
            hot_ref[pl.ds(2 * slot, 2), :] = (lane == spot).astype(jnp.float32)
            return carry

        lax.fori_loop(0, slots, body, 0)

    def sample():
        def body(group, carry):
            for rank in range(cap):
                slot = group * cap + rank
                row = lax.div(cells[rank, group], cz)
                for t, f in enumerate((0, 4)):
                    g_ref[pl.ds(2 * slot + t, 1), :] = s_ref[
                        0, f, lax.div(row, cy), pl.ds(PAD + lax.rem(row, cy), 1), :
                    ]
            return carry

        lax.fori_loop(0, groups, body, 0, unroll=min(groups, 8))
        heard = jnp.sum(jnp.where(hot_ref[...] != 0.0, g_ref[...], 0.0), axis=1, keepdims=True)
        heard = heard.astype(jnp.bfloat16).astype(jnp.float32)
        return jnp.broadcast_to(heard, g_ref.shape)

    def parcel_copy(offset):
        where_to = (me["cfd"] * sizes[2] + me["obs"] + offset) % (sizes[0] * sizes[2])
        c, z = where_to // sizes[2], where_to % sizes[2]
        return pltpu.make_async_remote_copy(
            src_ref=parcel_ref.at[z, c],
            dst_ref=w_ref.at[me["obs"] * sizes[0] + me["cfd"]],
            send_sem=w_sem.at[0],
            recv_sem=w_sem.at[1],
            device_id={"cfd": c, "panel": me["panel"], "obs": z},
            device_id_type=pl.DeviceIdType.MESH,
        )

    def result_copy(target):
        block = (target["obs"] * sizes[0] + target["cfd"]) * sizes[1] + target["panel"]
        return pltpu.make_async_remote_copy(
            src_ref=part_ref.at[block],
            dst_ref=gather_ref.at[my_index],
            send_sem=r_sem.at[0],
            recv_sem=r_sem.at[1],
            device_id=target,
            device_id_type=pl.DeviceIdType.MESH,
        )

    def turn(axis, offset):
        moved = me[axis] + offset
        return jnp.where(moved >= span[axis], moved - span[axis], moved)

    loads[0].wait()
    send(0, ("cfd",))
    pack_sides(0)
    send(0, ("panel",))
    packed = blank()
    for x in range(cx):
        for f in range(fields):
            packed = collect(packed, x, f, s_ref[0, f, x, PAD : PAD + cy, :])
    zs_ref[0] = packed
    send(0, ("obs",))
    for load in loads[1:]:
        load.wait()
    m_ref[...] = half * m_ref[...]
    visc_all = TIME_STEP * v_ref[...]
    v_ref[...] = visc_all
    vy_ref[0] = visc_all[:, 0, :]
    vy_ref[1] = visc_all[:, cy - 1, :]
    rims = blank()
    for x in range(cx):
        for f in range(fields):
            rims = collect(rims, x, f, visc_all[x])
    vz_ref[...] = rims

    observers = raw_ref.shape[3]
    parcel_ref[:, :, :, :observers] = raw_ref[...].astype(jnp.float32)
    rest = (raw_ref.shape[2], parcel_ref.shape[3] - observers)
    rest_lane = lax.broadcasted_iota(jnp.int32, rest, 1)
    for z in range(sizes[2]):

        @pl.loop(0, sizes[0])
        def _(c):
            value = jnp.zeros(rest, jnp.int32)
            for b in range(late_bins.shape[1]):
                value = jnp.where(rest_lane == b, late_bins[z, b, c], value)
            parcel_ref[z, c, :, observers:] = value.astype(jnp.float32)

    mark()
    group = sizes[0] * sizes[2]
    share = part_ref.shape[1]
    half_rows = part_ref.shape[0] * share // sizes[2]
    blocks = max(half_rows // 128, 1)
    block_rows = half_rows // blocks
    depth = 2 * slots
    bins = lax.broadcasted_iota(jnp.int32, (depth, part_ref.shape[2]), 1).astype(jnp.float32)

    def prepare():
        w_ref[me["obs"] * sizes[0] + me["cfd"]] = parcel_ref[me["obs"], me["cfd"]]
        whole = w_ref.at[pl.ds(0, group - 1)]
        pltpu.make_async_copy(whole, whole, w_sem.at[1]).wait()
        pltpu.make_async_copy(whole, whole, w_sem.at[0]).wait()
        for h in range(sizes[2]):
            held = slice(h * sizes[0], (h + 1) * sizes[0])
            for b in range(blocks):
                weight = w_ref[held, :, b * block_rows : (b + 1) * block_rows].reshape(depth, block_rows)
                delay = w_ref[held, :, half_rows + b : half_rows + b + 1].reshape(depth, 1)
                late = bins - delay
                spread = jnp.zeros(bins.shape, jnp.float32)
                for k in range(STEPS - 1):
                    spread = jnp.where(late == float(k), sig_ref[k], spread)
                wt_ref[h, b] = jnp.transpose(weight).astype(jnp.bfloat16)
                late_ref[h, b] = late
                early_ref[h, b] = spread

    @pl.loop(0, STEPS)
    def _(step):
        @pl.when(step == STEPS - 1)
        def _():
            @pl.loop(1, sizes[0] * sizes[2])
            def _(offset):
                parcel_copy(offset).start()

        for number in range(3):
            src, dst = number, (number + 1) % 3
            bulk(src, dst, number)
            if number == 2:

                @pl.when(step == STEPS - 1)
                def _():
                    prepare()

            settle(src)
            more = jnp.logical_or(step < STEPS - 1, number < 2)
            for axis in correct(src, dst, number):

                @pl.when(more)
                def _():
                    send(dst, (axis,))

            if number == 2:

                @pl.when(step < STEPS - 1)
                def _():
                    sig_ref[step] = sample()

    final = sample()
    for h in range(sizes[2]):
        for b in range(blocks):
            spread = jnp.where(late_ref[h, b] == float(STEPS - 1), final, early_ref[h, b])
            heard = lax.dot_general(
                wt_ref[h, b],
                spread.astype(jnp.bfloat16),
                (((1,), (0,)), ((), ())),
                preferred_element_type=jnp.float32,
            )
            first = (h * half_rows + b * block_rows) // share
            part_ref[first : first + block_rows // share] = heard.reshape(
                block_rows // share, share, part_ref.shape[2]
            )

    if total <= 64:
        hops = sorted(range(sizes[0]), key=lambda a: (a == 0, min(a, sizes[0] - a)))
        for a in hops:
            places = [(a, b, d) for b in reversed(range(sizes[1])) for d in reversed(range(sizes[2]))]
            for spots in places:
                if any(spots):
                    result_copy({axis: turn(axis, k) for axis, k in zip(AXES, spots)}).start()
    else:

        @pl.loop(1, total)
        def _(offset):
            result_copy(place((my_index + offset) % total)).start()

    flow_out[...] = s_ref[0, :, :, PAD : PAD + cy, :]
    own = (me["obs"] * sizes[0] + me["cfd"]) * sizes[1] + me["panel"]
    gather_ref[my_index] = part_ref[own]

    others = gather_ref.at[pl.ds(0, total - 1)]
    pltpu.make_async_copy(others, others, r_sem.at[1]).wait()
    heard_out[...] = jnp.sum(gather_ref[...], axis=0)

    pltpu.make_async_copy(others, others, r_sem.at[0]).wait()


def per_device(sizes, state, mean_speed, eddy_visc, panel_cell, panel_count, weights, delays):
    fields, cx, cy, cz = state.shape
    slots = panel_cell.shape[3] * panel_cell.shape[4]
    halves, sources, cap, kinds = weights.shape[1:5]
    observers = weights.shape[6]
    blocks = delays.shape[4]
    bins = 128
    width = -(-(observers + blocks) // 128) * 128
    deep = cap * kinds
    weight = weights.reshape(halves, sources, deep, observers)
    delay = delays.reshape(halves, sources, blocks).transpose(0, 2, 1)
    cell = panel_cell.reshape(panel_cell.shape[3:]).transpose(1, 0)
    total = sizes[0] * sizes[1] * sizes[2]
    share = observers // (sizes[0] * sizes[1])
    parts = max(observers // 128, 1)
    anywhere = pl.BlockSpec(memory_space=pl.ANY)
    scalar = pl.BlockSpec(memory_space=pltpu.SMEM)
    flow, heard = pl.pallas_call(
        functools.partial(window_kernel, sizes),
        out_shape=(
            pltpu.VMEM(state.shape, jnp.float32),
            pltpu.VMEM((share, bins), jnp.float32),
        ),
        in_specs=[scalar, scalar, scalar, anywhere, anywhere, anywhere, anywhere],
        out_specs=(pl.BlockSpec(memory_space=pltpu.VMEM),) * 2,
        scratch_shapes=[
            pltpu.VMEM((3, fields, cx, cy + 2 * PAD, cz), jnp.float32),
            pltpu.VMEM((3, 2, fields, cy, cz), jnp.float32),
            pltpu.VMEM((3, 2, fields, cx, cz), jnp.float32),
            pltpu.VMEM((3, 2, fields, cx, cz), jnp.float32),
            pltpu.VMEM((cx, cy, cz), jnp.float32),
            pltpu.VMEM((cx, cy, cz), jnp.float32),
            pltpu.VMEM((2, cx, cz), jnp.float32),
            pltpu.VMEM((cy, cz), jnp.float32),
            pltpu.VMEM((3, cy, cz), jnp.float32),
            pltpu.VMEM((3, cy, cz), jnp.float32),
            pltpu.VMEM((halves, sources, deep, observers), jnp.bfloat16),
            pltpu.VMEM((2 * slots, cz), jnp.float32),
            pltpu.VMEM((2 * slots, cz), jnp.float32),
            pltpu.VMEM((STEPS - 1, 2 * slots, bins), jnp.float32),
            pltpu.VMEM((halves, sources, deep, width), jnp.float32),
            pltpu.VMEM((halves * sources, deep, width), jnp.float32),
            pltpu.VMEM((halves, parts, observers // parts, 2 * slots), jnp.bfloat16),
            pltpu.VMEM((halves, parts, 2 * slots, bins), jnp.float32),
            pltpu.VMEM((halves, parts, 2 * slots, bins), jnp.float32),
            pltpu.VMEM((total, share, bins), jnp.float32),
            pltpu.VMEM((total, share, bins), jnp.float32),
            pltpu.SemaphoreType.DMA((4,)),
            pltpu.SemaphoreType.DMA((3, 6)),
            pltpu.SemaphoreType.DMA((3, 6)),
            pltpu.SemaphoreType.DMA((2,)),
            pltpu.SemaphoreType.DMA((2,)),
        ],
        compiler_params=pltpu.CompilerParams(collective_id=0, has_side_effects=True),
        name="window",
    )(cell, panel_count.reshape(-1), delay, state, mean_speed, eddy_visc, weight)
    return flow, heard[None]


def solution(mesh):
    in_specs = (
        P(None, "cfd", "panel", "obs"),
        P("cfd", "panel", "obs"),
        P("cfd", "panel", "obs"),
        P("cfd", "panel", "obs", None, None),
        P("cfd", "panel", "obs", None),
        P(("cfd", "panel"), None, None, None, None, "obs", None),
        P(("cfd", "panel"), None, None, "obs", None),
    )
    out_specs = (P(None, "cfd", "panel", "obs"), P("obs", ("cfd", "panel"), None))
    sizes = tuple(mesh.shape[axis] for axis in AXES)
    return jax.shard_map(
        functools.partial(per_device, sizes),
        mesh=mesh,
        in_specs=in_specs,
        out_specs=out_specs,
        check_vma=False,
    )
```

profile of v0, /device:TPU:0, one launch (start us, length us, event | category | flops | bytes accessed | tf_op | source)
XLA Modules:
  0.0 50.2 jit_solution(6444256009618914379)
XLA Ops:
  0.6 48.3 %window.1 = (f32[5,8,16,128]{3,2,1,0:T(8,128)S(1)}, f32[4,128]{1,0:T(4,128)S(1)}) custom-call(s32[4,8]{1,0:T(4,128)} %bitcast.11, s32[8]{0:T(128)} %bitcast.13, s32[2,1,8]{2,1,0:T(1,128)} %bitcast.12, f32[5,8,16,128]{3,2,1,0:T(8,128)} %state.1, f32[8,16,128]{2,1,0:T(8,128)} %speed.1, f32[8,16,128]{2,1,0:T(8,128)} %visc.1, bf16[2,8,8,64]{3,2,1,0:T(8,128)(2,1)} %bitcast.10), custom_call_target="tpu_custom_call" | custom-call | tf_op jit(solution)/shard_map/window/pallas_call | solution.py:516
  48.9 0.7 %copy.12 = f32[5,8,16,128]{3,2,1,0:T(8,128)} copy(f32[5,8,16,128]{3,2,1,0:T(8,128)S(1)} %get-tuple-element.6) | data formatting | bytes 655360
  49.7 0.6 %copy.13 = f32[1,4,128]{2,1,0:T(4,128)} copy(f32[1,4,128]{2,1,0:T(4,128)S(1)} %bitcast.9) | data formatting | bytes 4096
where the time goes:
time: 50.4 us; the launch traced here: 50.2 us
  Pallas kernels  48.3 us (96%)
  local copies, waits for them, and re-layouts  1.3 us (3%)
  between operations  0.64 us (1%)
    pallas_call x1, Pallas kernels, per_device(): pl.pallas_call(functools.partial(window_kernel, sizes), out_shape=(pltpu....  48.3 us
    unnamed x2, local copies, waits for them, and re-layouts  1.3 us

commit v1 on v0

--- a/solution.py
+++ b/solution.py
@@ -28,11 +28,13 @@
     hx_ref,
     hy_ref,
     ys_ref,
+    yb_ref,
     m_ref,
     v_ref,
     vy_ref,
     vz_ref,
     zs_ref,
+    zb_ref,
     zr_ref,
     raw_ref,
     g_ref,
@@ -121,9 +123,8 @@
 
             @pl.when(jnp.logical_not(has[axis, way]))
             def _():
-                halo[:, side] = jnp.zeros((3,) + halo.shape[2:], jnp.float32)
-
-    zs_ref[...] = jnp.zeros(zs_ref.shape, jnp.float32)
+                halo[:, side] = jnp.zeros((3,) + halo.shape[2:], halo.dtype)
+
 
     def route(buf, axis, way):
         side = 0 if way == 1 else 1
@@ -131,10 +132,10 @@
             src = s_ref.at[buf, :, cx - 1 if way == 1 else 0, pl.ds(PAD, cy), :]
             dst = hx_ref.at[buf, side]
         elif axis == "panel":
-            src = ys_ref.at[buf, 1 - side]
+            src = yb_ref.at[buf, 1 - side]
             dst = hy_ref.at[buf, side]
         else:
-            src = zs_ref.at[buf]
+            src = zb_ref.at[buf]
             dst = zr_ref.at[buf]
         lane = 2 * AXES.index(axis) + (way == 1)
         return pltpu.make_async_remote_copy(
@@ -185,7 +186,19 @@
     def pack_sides(buf):
         for f in range(fields):
             for side, row in enumerate((PAD, PAD + cy - 1)):
-                ys_ref[buf, side, f] = s_ref[buf, f, :, row, :]
+                ys_ref[side, f] = s_ref[buf, f, :, row, :]
+
+    def put_side(buf, side, parts):
+        rest = jnp.zeros((yb_ref.shape[2] - fields * cx, cz), jnp.float32)
+        tall = jnp.concatenate(parts + ([rest] if rest.shape[0] else []), axis=0)
+        yb_ref[buf, side] = tall.astype(yb_ref.dtype)
+
+    def fill_sides(buf):
+        for side, row in enumerate((PAD, PAD + cy - 1)):
+            put_side(buf, side, [s_ref[buf, f, :, row, :] for f in range(fields)])
+
+    def put_rim(buf, value):
+        zb_ref[buf] = value.astype(zb_ref.dtype)
 
     def blank():
         return jnp.zeros((cy, cz), jnp.float32)
@@ -231,7 +244,7 @@
                     value = s_ref[0, f, x, PAD : PAD + cy, :] * (1.0 / 3.0) + (2.0 / 3.0) * value
                 s_ref[dst, f, x, PAD : PAD + cy, :] = value
                 packed = collect(packed, x, f, value)
-        zs_ref[dst] = packed
+        zs_ref[...] = packed
         pack_sides(dst)
 
     sub_id = lax.broadcasted_iota(jnp.int32, (8, cz), 0)
@@ -245,10 +258,13 @@
         base[normal] = base[normal] + sent * halo[4]
         return base
 
+    def split(tall):
+        return [tall[f * cx : (f + 1) * cx] for f in range(fields)]
+
     def correct(src, dst, number):
         scale = (1.0, 0.25, 2.0 / 3.0)[number]
         south, north = [
-            push([hy_ref[src, side, f] for f in range(fields)], vy_ref[side], way, 2, scale)
+            push(split(hy_ref[src, side].astype(jnp.float32)), vy_ref[side], way, 2, scale)
             for side, way in enumerate((-1, 1))
         ]
         faces = {}
@@ -259,7 +275,7 @@
         step_id = lax.broadcasted_iota(jnp.int32, (cx, cz), 0)
         end = jnp.where(low, 0, cz - 1)
         sent = jnp.where(low, half * scale, -half * scale)
-        held = zr_ref[src]
+        held = zr_ref[src].astype(jnp.float32)
         cross = jnp.where(
             lane_id < cx,
             pltpu.roll(held, cz - 3 * cx, 1),
@@ -267,6 +283,17 @@
         )
         crossed = (lane_id < cx) | ((lane_id >= 3 * cx) & (lane_id < 5 * cx))
         fix = (scale * vz_ref[...]) * held + sent * jnp.where(crossed, cross, 0.0)
+        turned = jnp.transpose(fix)
+        for side, (own, row) in enumerate(((south, 0), (north, cy - 1))):
+            parts = []
+            for f in range(fields):
+                ends = turned[f * cx : (f + 1) * cx, row : row + 1]
+                side_fix = own[f] + jnp.where(spot == end, ends, 0.0)
+                for x in (0, cx - 1):
+                    side_fix = side_fix + jnp.where(step_id == x, faces[x][f][row : row + 1, :], 0.0)
+                parts.append(ys_ref[side, f] + side_fix)
+            put_side(dst, side, parts)
+        yield "panel"
         tall = jnp.zeros((cy, cz), jnp.float32)
         for x in (0, cx - 1):
             for f in range(fields):
@@ -279,17 +306,8 @@
             rows_out.append(jnp.sum(wide, axis=0, keepdims=True))
         tall = tall + jnp.where(row_id == 0, rows_out[0], 0.0)
         tall = tall + jnp.where(row_id == cy - 1, rows_out[1], 0.0)
-        zs_ref[dst] = zs_ref[dst] + (fix + tall)
+        put_rim(dst, zs_ref[...] + (fix + tall))
         yield "obs"
-        turned = jnp.transpose(fix)
-        for side, (own, row) in enumerate(((south, 0), (north, cy - 1))):
-            for f in range(fields):
-                ends = turned[f * cx : (f + 1) * cx, row : row + 1]
-                side_fix = own[f] + jnp.where(spot == end, ends, 0.0)
-                for x in (0, cx - 1):
-                    side_fix = side_fix + jnp.where(step_id == x, faces[x][f][row : row + 1, :], 0.0)
-                ys_ref[dst, side, f] = ys_ref[dst, side, f] + side_fix
-        yield "panel"
         for place_x, x in enumerate([0, cx - 1] + list(range(1, cx - 1))):
             for f in range(fields):
                 rim = [jnp.where(sub_id == 0, south[f][x : x + 1, :], 0.0)]
@@ -364,15 +382,13 @@
         return jnp.where(moved >= span[axis], moved - span[axis], moved)
 
     loads[0].wait()
-    send(0, ("cfd",))
-    pack_sides(0)
-    send(0, ("panel",))
+    fill_sides(0)
     packed = blank()
     for x in range(cx):
         for f in range(fields):
             packed = collect(packed, x, f, s_ref[0, f, x, PAD : PAD + cy, :])
-    zs_ref[0] = packed
-    send(0, ("obs",))
+    put_rim(0, packed)
+    send(0, ("panel", "obs", "cfd"))
     for load in loads[1:]:
         load.wait()
     m_ref[...] = half * m_ref[...]
@@ -445,11 +461,12 @@
 
             settle(src)
             more = jnp.logical_or(step < STEPS - 1, number < 2)
-            for axis in correct(src, dst, number):
+            for axes in correct(src, dst, number):
+                axes = axes if isinstance(axes, tuple) else (axes,)
 
                 @pl.when(more)
                 def _():
-                    send(dst, (axis,))
+                    send(dst, axes)
 
             if number == 2:
 
@@ -511,6 +528,7 @@
     total = sizes[0] * sizes[1] * sizes[2]
     share = observers // (sizes[0] * sizes[1])
     parts = max(observers // 128, 1)
+    tall = -(-fields * cx // 16) * 16
     anywhere = pl.BlockSpec(memory_space=pl.ANY)
     scalar = pl.BlockSpec(memory_space=pltpu.SMEM)
     flow, heard = pl.pallas_call(
@@ -524,14 +542,16 @@
         scratch_shapes=[
             pltpu.VMEM((3, fields, cx, cy + 2 * PAD, cz), jnp.float32),
             pltpu.VMEM((3, 2, fields, cy, cz), jnp.float32),
-            pltpu.VMEM((3, 2, fields, cx, cz), jnp.float32),
-            pltpu.VMEM((3, 2, fields, cx, cz), jnp.float32),
+            pltpu.VMEM((3, 2, tall, cz), jnp.bfloat16),
+            pltpu.VMEM((2, fields, cx, cz), jnp.float32),
+            pltpu.VMEM((3, 2, tall, cz), jnp.bfloat16),
             pltpu.VMEM((cx, cy, cz), jnp.float32),
             pltpu.VMEM((cx, cy, cz), jnp.float32),
             pltpu.VMEM((2, cx, cz), jnp.float32),
             pltpu.VMEM((cy, cz), jnp.float32),
-            pltpu.VMEM((3, cy, cz), jnp.float32),
-            pltpu.VMEM((3, cy, cz), jnp.float32),
+            pltpu.VMEM((cy, cz), jnp.float32),
+            pltpu.VMEM((3, cy, cz), jnp.bfloat16),
+            pltpu.VMEM((3, cy, cz), jnp.bfloat16),
             pltpu.VMEM((halves, sources, deep, observers), jnp.bfloat16),
             pltpu.VMEM((2 * slots, cz), jnp.float32),
             pltpu.VMEM((2 * slots, cz), jnp.float32),

time: 50.4 us -> 49.2 us (0.976)
  Pallas kernels: 48.3 us -> 47.1 us
    pallas_call x1, Pallas kernels: 48.3 us -> 47.1 us  [per_device(): pl.pallas_call(functools.partial(window_kernel, sizes), out_shape=(pltpu....]
where the time goes in v1:
time: 49.2 us; the launch traced here: 49.1 us
  Pallas kernels  47.1 us (96%)
  local copies, waits for them, and re-layouts  1.3 us (3%)
  between operations  0.64 us (1%)
    pallas_call x1, Pallas kernels, per_device(): pl.pallas_call(functools.partial(window_kernel, sizes), out_shape=(pltpu....  47.1 us
    unnamed x2, local copies, waits for them, and re-layouts  1.3 us

profile of v1, /device:TPU:0, one launch (start us, length us, event | category | flops | bytes accessed | tf_op | source)
XLA Modules:
  0.0 49.1 jit_solution(17350561679442321840)
XLA Ops:
  0.6 47.1 %window.1 = (f32[5,8,16,128]{3,2,1,0:T(8,128)S(1)}, f32[4,128]{1,0:T(4,128)S(1)}) custom-call(s32[4,8]{1,0:T(4,128)} %bitcast.11, s32[8]{0:T(128)} %bitcast.13, s32[2,1,8]{2,1,0:T(1,128)} %bitcast.12, f32[5,8,16,128]{3,2,1,0:T(8,128)} %state.1, f32[8,16,128]{2,1,0:T(8,128)} %speed.1, f32[8,16,128]{2,1,0:T(8,128)} %visc.1, bf16[2,8,8,64]{3,2,1,0:T(8,128)(2,1)} %bitcast.10), custom_call_target="tpu_custom_call" | custom-call | tf_op jit(solution)/shard_map/window/pallas_call | solution.py:534
  47.8 0.7 %copy.12 = f32[5,8,16,128]{3,2,1,0:T(8,128)} copy(f32[5,8,16,128]{3,2,1,0:T(8,128)S(1)} %get-tuple-element.6) | data formatting | bytes 655360
  48.5 0.6 %copy.13 = f32[1,4,128]{2,1,0:T(4,128)} copy(f32[1,4,128]{2,1,0:T(4,128)S(1)} %bitcast.9) | data formatting | bytes 4096
